TPU v7x, 32 devices: a whole 2x2x4 slice. The times are simulated.
32 devices in a mesh: req: 4 (over y, core), seq: 8 (over z, x).
Axes of the slice: x: 2, y: 2, z: 4, core: 2. Of those that a mesh axis runs over, the one named last changes fastest.
Arguments:
- embedded: bfloat16 [4, 48, 3584], P(None, 'req'), may hold values from -6 to 6
- cache_keys: bfloat16 [4, 4096, 2048], P('req', 'seq'), may hold values from -6 to 6
- cache_values: bfloat16 [4, 4096, 2048], P('req', 'seq'), may hold values from -6 to 6
- token_owner: int32 [4, 4096], P('req', 'seq'), may hold values from 0 to 11, as said below
- dealing: int32 [48], replicated, may hold values from 0 to 47, as said below
- lengths: int32 [48], replicated, may hold values from 1 to 2048, as said below
- project_weight: bfloat16 [3584, 8192], P(None, 'seq')
- output_weight: bfloat16 [4096, 3584], P('seq'), may hold values from -0.09375 to 0.09375
- gate_weight: bfloat16 [3584, 14336], P(None, ('req', 'seq')), may hold values from -0.09375 to 0.09375
- up_weight: bfloat16 [3584, 14336], P(None, ('req', 'seq')), may hold values from -0.09375 to 0.09375
- down_weight: bfloat16 [14336, 3584], P(('req', 'seq')), may hold values from -0.046875 to 0.046875
- gain_first: float32 [3584], replicated, may hold values from 0.1 to 1.9
- gain_second: float32 [3584], replicated, may hold values from 0.1 to 1.9
- gain_third: float32 [3584], replicated, may hold values from 0.1 to 1.9
- gain_fourth: float32 [3584], replicated, may hold values from 0.1 to 1.9
Outputs:
- results: bfloat16 [4, 48, 3584], P(None, 'req')
Inputs may be any that keep to these rules, and one draw needn't show every extreme that they name: A permutation of the requests; slot i of req group g serves request dealing[g * 12 + i]. The lengths of the 12 requests dealt to one group sum to 4096; in every group the longest is exactly 2048. `token_owner`: each slot owns a contiguous run of its group's pool, runs in slot order, as many tokens as its request's length.
All inputs are finite; a program needn't handle non-finite values.
Results may differ from a plain program's by a relative error of at most 0.012.
The roundings to bfloat16 on the way count: a program that leaves them out, or rounds other values in their place, can miss the bound.
Values may be sent and summed in bfloat16 or wider, within the bound.
A program may use at most 128 MiB of HBM per device.

v0:
```python
import math
import jax
import jax.numpy as jnp
from jax import lax
from jax.sharding import PartitionSpec as P

H = 16
KVH = 8
HD = 256
STEPS = 4
soft_cap = 50.0
epsilon = 1e-06


def rms_scale(values, gain):
    mean_square = jnp.mean(values * values, axis=-1, keepdims=True)
    return values * lax.rsqrt(mean_square + epsilon) * gain


def rotate(values, positions):
    half_width = values.shape[-1] // 2
    freq_index = jnp.arange(half_width, dtype=jnp.float32)
    inverse = jnp.exp(freq_index * (-2.0 * math.log(10000.0) / values.shape[-1]))
    angles = positions[:, None] * inverse[None, :]
    cosine = jnp.cos(angles)[:, None, :]
    sine = jnp.sin(angles)[:, None, :]
    first_half = values[..., :half_width]
    second_half = values[..., half_width:]
    return jnp.concatenate(
        [first_half * cosine - second_half * sine, second_half * cosine + first_half * sine],
        axis=-1,
    )


def capped_weight(scores):
    return jnp.exp(soft_cap * jnp.tanh(scores / soft_cap))


def rounded(values):
    return lax.optimization_barrier(values.astype(jnp.bfloat16)).astype(jnp.float32)


def body(
    embedded,
    cache_keys,
    cache_values,
    token_owner,
    dealing,
    lengths,
    project_weight,
    output_weight,
    gate_weight,
    up_weight,
    down_weight,
    gain_first,
    gain_second,
    gain_third,
    gain_fourth,
):
    row_count = embedded.shape[1]
    rows = STEPS * row_count
    width = embedded.shape[2]
    local_tokens = cache_keys.shape[1]
    value_width = cache_keys.shape[2]
    group_size = H // KVH
    attention_width = H * HD
    column_count = output_weight.shape[0]
    group_index = lax.axis_index("req")
    seq_index = lax.axis_index("seq")
    seq_size = lax.axis_size("seq")
    req_size = lax.axis_size("req")
    column_start = seq_index * column_count
    slot_requests = lax.dynamic_slice_in_dim(dealing, group_index * row_count, row_count)
    matches = slot_requests[:, None] == jnp.arange(dealing.shape[0], dtype=jnp.int32)[None, :]
    base_positions = jnp.sum(jnp.where(matches, lengths[None, :], 0), axis=1)
    positions = base_positions[None, :] + jnp.arange(STEPS, dtype=jnp.int32)[:, None]
    positions = positions.reshape(rows).astype(jnp.float32)
    key_pool = cache_keys[0].reshape(local_tokens, KVH, HD)
    value_pool = cache_values[0].reshape(local_tokens, KVH, HD)
    slots = jnp.tile(jnp.arange(row_count, dtype=jnp.int32), STEPS)
    moments = jnp.repeat(jnp.arange(STEPS, dtype=jnp.int32), row_count)
    owned_mask = token_owner[0][None, :] == slots[:, None]
    stream = embedded.reshape(rows, width).astype(jnp.float32)
    normed = rms_scale(stream, gain_first).astype(jnp.bfloat16)
    local_part = jnp.dot(normed, project_weight, preferred_element_type=jnp.float32).astype(
        jnp.bfloat16
    )
    projected = lax.all_gather(local_part, "seq", axis=1, tiled=True)
    query_rows = projected[:, :attention_width].astype(jnp.float32).reshape(rows, H, HD)
    queries = (rotate(query_rows, positions) * HD ** (-0.5)).astype(jnp.bfloat16)
    key_rows = (
        projected[:, attention_width : attention_width + value_width]
        .astype(jnp.float32)
        .reshape(rows, KVH, HD)
    )
    fresh_keys = rotate(key_rows, positions).astype(jnp.bfloat16)
    fresh_values = projected[:, attention_width + value_width :].reshape(rows, KVH, HD)
    grouped = queries.reshape(rows, KVH, group_size, HD)
    all_keys = jnp.concatenate([key_pool, fresh_keys], axis=0)
    all_values = jnp.concatenate([value_pool, fresh_values], axis=0)
    fresh_mask = (
        (slots[None, :] == slots[:, None])
        & (moments[None, :] <= moments[:, None])
        & (seq_index == 0)
    )
    mask = jnp.concatenate([owned_mask, fresh_mask], axis=1)
    scores = jnp.einsum("igqd,tgd->igqt", grouped, all_keys, preferred_element_type=jnp.float32)
    weights = jnp.where(mask[:, None, None, :], capped_weight(scores), 0.0)
    totals = lax.psum(jnp.sum(weights, axis=-1), "seq").reshape(rows, H)
    outputs = jnp.einsum(
        "igqt,tgd->igqd",
        weights.astype(jnp.bfloat16),
        all_values,
        preferred_element_type=jnp.float32,
    ).reshape(rows, attention_width)
    outputs = lax.psum_scatter(outputs, "seq", scatter_dimension=1, tiled=True)
    spread = jnp.repeat(totals, HD, axis=1)
    spread = lax.dynamic_slice_in_dim(spread, column_start, column_count, 1)
    attended = (outputs / spread).astype(jnp.bfloat16)
    partial = jnp.dot(attended, output_weight, preferred_element_type=jnp.float32)
    mixed = lax.psum(partial, "seq")
    middle = stream + rms_scale(mixed, gain_second)
    feed_input = rms_scale(middle, gain_third).astype(jnp.bfloat16)
    block_rows = lax.all_gather(feed_input, "req", axis=0, tiled=True)
    gate_part = jnp.dot(block_rows, gate_weight, preferred_element_type=jnp.float32)
    up_part = jnp.dot(block_rows, up_weight, preferred_element_type=jnp.float32)
    hidden = (jax.nn.gelu(gate_part, approximate=True) * up_part).astype(jnp.bfloat16)
    summed = jnp.dot(hidden, down_weight, preferred_element_type=jnp.float32)
    summed = lax.psum_scatter(summed, "req", scatter_dimension=0, tiled=True)
    summed = lax.psum(summed, "seq")
    results = (middle + rms_scale(summed, gain_fourth)).astype(jnp.bfloat16)
    return results.reshape(STEPS, row_count, width)


def solution(mesh):
    return jax.shard_map(
        body,
        mesh=mesh,
        in_specs=(
            P(None, "req", None),
            P("req", "seq", None),
            P("req", "seq", None),
            P("req", "seq"),
            P(),
            P(),
            P(None, "seq"),
            P("seq", None),
            P(None, ("req", "seq")),
            P(None, ("req", "seq")),
            P(("req", "seq"), None),
            P(),
            P(),
            P(),
            P(),
        ),
        out_specs=P(None, "req", None),
        check_vma=False,
    )
```

profile of v0, /device:TPU:0, one launch (start us, length us, event | category | flops | bytes accessed | tf_op | source)
XLA Modules:
  0.0 383.3 jit_solution(17114336762805842567)
XLA Ops:
  6.6 2.1 copy.64
  9.9 2.1 reshape.160
  12.2 4.8 %convolution_convert_fusion = bf16[48,1024]{1,0:T(8,128)(2,1)S(1)} fusion(bf16[3584,1024]{1,0:T(8,128)(2,1)} %param.21, f32[48,3584]{1,0:T(8,128)} %reshape.160, f32[3584]{0:T(1024)S(1)} %copy-done.4, f32[48]{0:T(128)S(1)} %rsqrt.36), kind=kOutput, calls=%fused_computation.14 | convolution fusion | flops 352886784 | bytes 8140992 | tf_op jit(solution)/shard_map/dot_general | solution.py:85
  17.0 33.8 %all_gather.6 = bf16[48,8192]{1,0:T(8,128)(2,1)S(1)} all-gather(bf16[48,1024]{1,0:T(8,128)(2,1)S(1)} %convolution_convert_fusion), channel_id=1, replica_groups=mesh['req'=4,'seq'=8] {'seq'}, dimensions={1}, use_global_device_ids=true | all-gather | bytes 884736 | tf_op jit(solution)/shard_map/all_gather | solution.py:88
  58.6 3.9 %copy.69 = bf16[1,512,2048]{1,2,0:T(8,128)(2,1)} copy(bf16[1,512,2048]{2,1,0:T(8,128)(2,1)} %param.16) | data formatting | bytes 4194304 | tf_op args[1]
  62.6 3.9 %copy.72 = bf16[512,8,256]{2,0,1:T(8,128)(2,1)} copy(bf16[512,8,256]{0,2,1:T(8,128)(2,1)} %bitcast.44) | data formatting | bytes 4194304 | tf_op jit(solution)/shard_map/reshape;squeeze | solution.py:78
  66.5 1.6 copy.92
  68.1 3.9 %copy.65 = bf16[1,512,2048]{1,2,0:T(8,128)(2,1)} copy(bf16[1,512,2048]{2,1,0:T(8,128)(2,1)} %param.17) | data formatting | bytes 4194304 | tf_op args[2]
  72.0 3.9 %copy.67 = bf16[512,8,256]{2,0,1:T(8,128)(2,1)} copy(bf16[512,8,256]{0,2,1:T(8,128)(2,1)} %bitcast.45) | data formatting | bytes 4194304 | tf_op jit(solution)/shard_map/reshape;squeeze | solution.py:79
  77.0 2.9 fusion.40
  80.5 1.5 copy.75
  82.1 2.6 reshape.156
  84.8 21.7 %psum.21 = f32[48,16]{0,1:T(8,128)S(1)} all-reduce(f32[48,16]{0,1:T(8,128)S(1)} %bitcast.56), channel_id=1, replica_groups=mesh['req'=4,'seq'=8] {'seq'}, use_global_device_ids=true, to_apply=%region_4.5 | all-reduce | flops 768 | bytes 6144 | tf_op jit(solution)/shard_map/psum | solution.py:109
  108.1 40.9 %reduce-scatter.3.cloned.1.call-done = f32[48,512]{1,0:T(8,128)} async-done(((f32[48,4096]{1,0:T(8,128)}), f32[48,512]{1,0:T(8,128)}) %reduce-scatter.3.cloned.1.call-update) | async-done | bytes 98320 | tf_op jit(solution)/shard_map/reduce_scatter | solution.py:116
  149.0 3.8 fusion.29
  152.8 72.8 %all-reduce.3.cloned.1.call-done = f32[48,3584]{1,0:T(8,128)} async-done(((f32[48,3584]{1,0:T(8,128)}), f32[48,3584]{1,0:T(8,128)}) %all-reduce.3.cloned.1.call-update) | async-done | bytes 688144 | tf_op jit(solution)/shard_map/psum | solution.py:121
  226.9 1.6 multiply_reduce_fusion.1
  230.3 17.7 %all-gather.2.cloned.1.call-done = bf16[192,3584]{1,0:T(8,128)(2,1)} async-done(((bf16[48,3584]{1,0:T(8,128)(2,1)}), bf16[192,3584]{1,0:T(8,128)(2,1)}) %all-gather.2.cloned.1.call-update) | async-done | bytes 1376272 | tf_op jit(solution)/shard_map/all_gather | solution.py:124
  247.9 4.1 %fusion.41 = f32[192,448]{1,0:T(8,128)} fusion(bf16[192,3584]{1,0:T(8,128)(2,1)} %all-gather.2.cloned.1.call-done, bf16[3584,448]{0,1:T(8,128)(2,1)} %param.23), kind=kOutput, calls=%fused_computation.75 | convolution fusion | flops 616562688 | bytes 4931584 | tf_op jit(solution)/shard_map/dot_general | solution.py:125
  252.1 6.0 %fusion.10 = f32[192,3584]{1,0:T(8,128)} fusion(bf16[448,3584]{1,0:T(8,128)(2,1)S(1)} %copy-done, bf16[192,3584]{1,0:T(8,128)(2,1)} %all-gather.2.cloned.1.call-done, bf16[3584,448]{0,1:T(8,128)(2,1)} %param.24, f32[192,448]{1,0:T(8,128)} %fusion.41), kind=kOutput, calls=%fused_computation.15 | convolution fusion | flops 1233985536 | bytes 10895360 | tf_op jit(solution)/shard_map/dot_general | solution.py:128
  258.2 35.6 %reduce-scatter.5.cloned.1.call-done = f32[48,3584]{1,0:T(8,128)} async-done(((f32[192,3584]{1,0:T(8,128)}), f32[48,3584]{1,0:T(8,128)}) %reduce-scatter.5.cloned.1.call-update) | async-done | bytes 688144 | tf_op jit(solution)/shard_map/reduce_scatter | solution.py:129
  293.8 77.4 %all-reduce.5.cloned.1.call-done = f32[48,3584]{1,0:T(8,128)} async-done(((f32[48,3584]{1,0:T(8,128)}), f32[48,3584]{1,0:T(8,128)}) %all-reduce.5.cloned.1.call-update) | async-done | bytes 688144 | tf_op jit(solution)/shard_map/psum | solution.py:130
  372.4 1.5 add_convert_fusion
  374.7 2.0 copy.77
  (68 shorter events, 17.7 us)
Async XLA Ops:
  6.5 245.5 %copy-start = (bf16[448,3584]{1,0:T(8,128)(2,1)S(1)}, bf16[448,3584]{1,0:T(8,128)(2,1)}, u32[]{:S(2)}) copy-start(bf16[448,3584]{1,0:T(8,128)(2,1)} %param.25) | copy-start | bytes 9633796
  6.5 5.7 %copy-start.4 = (f32[3584]{0:T(1024)S(1)}, f32[3584]{0:T(1024)}, u32[]{:S(2)}) copy-start(f32[3584]{0:T(1024)} %param.26) | copy-start | bytes 43012
  6.5 142.4 %reduce-scatter.3.cloned.1.call-start = ((), (), s32[]{:S(2)}) async-start(), calls=%async_computation.2 | async-start | bytes 884736 | tf_op jit(solution)/shard_map/reduce_scatter | solution.py:116
  17.0 35.6 %copy-start.8 = (s32[48]{0:T(128)S(1)}, s32[48]{0:T(128)}, u32[]{:S(2)}) copy-start(s32[48]{0:T(128)} %param.19) | copy-start | bytes 580
  17.0 35.7 %copy-start.9 = (s32[48]{0:T(128)S(1)}, s32[48]{0:T(128)}, u32[]{:S(2)}) copy-start(s32[48]{0:T(128)} %param.20) | copy-start | bytes 580
  54.9 3.6 copy-start.7
  77.0 2.9 copy-start.2
  77.0 2.9 copy-start.3
  84.7 140.9 %all-reduce.3.cloned.1.call-start = ((), (), s32[]{:S(2)}) async-start(), calls=%async_computation.3 | async-start | bytes 1376256 | tf_op jit(solution)/shard_map/psum | solution.py:121
  149.0 77.9 %copy-start.6 = (f32[3584]{0:T(1024)S(1)}, f32[3584]{0:T(1024)}, u32[]{:S(2)}) copy-start(f32[3584]{0:T(1024)} %param.27) | copy-start | bytes 43012
  152.7 76.6 %copy-start.5 = (f32[3584]{0:T(1024)S(1)}, f32[3584]{0:T(1024)}, u32[]{:S(2)}) copy-start(f32[3584]{0:T(1024)} %param.28) | copy-start | bytes 43012
  152.7 95.2 %all-gather.2.cloned.1.call-start = ((), (), s32[]{:S(2)}) async-start(), calls=%async_computation.4 | async-start | bytes 1720320 | tf_op jit(solution)/shard_map/all_gather | solution.py:124
  228.4 0.9 copy-start.1
  230.2 63.5 %reduce-scatter.5.cloned.1.call-start = ((), (), s32[]{:S(2)}) async-start(), calls=%async_computation.5 | async-start | bytes 3440640 | tf_op jit(solution)/shard_map/reduce_scatter | solution.py:129
  258.1 113.0 %all-reduce.5.cloned.1.call-start = ((), (), s32[]{:S(2)}) async-start(), calls=%async_computation.6 | async-start | bytes 1376256 | tf_op jit(solution)/shard_map/psum | solution.py:130
Sparse Core Ops, SparseCore 0:
  84.8 64.0 reduce-scatter.2
  152.9 72.6 all-reduce.2
  230.3 17.5 all-gather.1
  258.2 35.4 reduce-scatter.4
  297.4 73.6 all-reduce.4
where the time goes:
time: 384 us; the launch traced here: 383 us
  waiting for transfers between devices  244 us (64%)
  blocking collectives  55.5 us (14%)
  local copies, waits for them, and re-layouts  36.6 us (10%)
  matrix products  22.2 us (6%)
  between operations  13.3 us (3%)
  other arithmetic  11.1 us (3%)
    psum x1, waiting for transfers between devices, body(): summed = lax.psum(summed, 'seq')  77.4 us
    psum x1, waiting for transfers between devices, body(): mixed = lax.psum(partial, 'seq')  72.8 us
    reduce_scatter x1, waiting for transfers between devices, body(): outputs = lax.psum_scatter(outputs, 'seq', scatter_dimension=1, tiled=True)  40.9 us
    reduce_scatter x1, waiting for transfers between devices, body(): summed = lax.psum_scatter(summed, 'req', scatter_dimension=0, tiled=True)  35.6 us
    all_gather x1, blocking collectives, body(): projected = lax.all_gather(local_part, 'seq', axis=1, tiled=True)  33.8 us
    psum x1, blocking collectives, body(): totals = lax.psum(jnp.sum(weights, axis=-1), 'seq').reshape(rows, H)  21.7 us
    all_gather x1, waiting for transfers between devices, body(): block_rows = lax.all_gather(feed_input, 'req', axis=0, tiled=True)  17.7 us
    unnamed x26, local copies, waits for them, and re-layouts  12.7 us
  transfers between devices with their start and end apart: 5, of which 5 were waited for; matrix products, arithmetic and copies ran while one was open for 0% of the time, Pallas kernels for 0%

commit v1 on v0

--- a/solution.py
+++ b/solution.py
@@ -85,7 +85,14 @@
     local_part = jnp.dot(normed, project_weight, preferred_element_type=jnp.float32).astype(
         jnp.bfloat16
     )
-    projected = lax.all_gather(local_part, "seq", axis=1, tiled=True)
+    built, out_arr = (lax.axis_size("seq"), lax.axis_index("seq"))
+    projected, g_now = (local_part, 1)
+    while g_now < built:
+        later = lax.ppermute(projected, "seq", [(j0, j0 ^ g_now) for j0 in range(built)])
+        after = jnp.concatenate([projected, later], 1)
+        part_next = jnp.concatenate([later, projected], 1)
+        projected = jnp.where(out_arr & g_now == 0, after, part_next)
+        g_now = 2 * g_now
     query_rows = projected[:, :attention_width].astype(jnp.float32).reshape(rows, H, HD)
     queries = (rotate(query_rows, positions) * HD ** (-0.5)).astype(jnp.bfloat16)
     key_rows = (

time: 384 us -> 358 us (0.932)
  blocking collectives: 55.5 us -> 21 us
  starting transfers between devices: 0.17 us -> 7.65 us
  waiting for transfers between devices: 244 us -> 251 us
  local copies, waits for them, and re-layouts: 36.6 us -> 32.3 us
    all_gather x1 -> x0, blocking collectives: 33.8 us -> none  [body(): projected = lax.all_gather(local_part, 'seq', axis=1, tiled=True)]
    ppermute x0 -> x3, starting transfers between devices: none -> 7.48 us  [body(): lax.ppermute(projected, 'seq', [(j0, j0 ^ g_now) for j0 in range(built)])]
    ppermute x0 -> x3, waiting for transfers between devices: none -> 6.9 us  [body(): lax.ppermute(projected, 'seq', [(j0, j0 ^ g_now) for j0 in range(built)])]
  transfers between devices with their start and end apart: 5 -> 8, of which waited for: 5 -> 8; matrix products, arithmetic and copies ran while one was open for 0% -> 5% of each run, Pallas kernels for 0% -> 0%
where the time goes in v1:
time: 358 us; the launch traced here: 357 us
  waiting for transfers between devices  251 us (70%)
  local copies, waits for them, and re-layouts  32.3 us (9%)
  blocking collectives  21 us (6%)
  matrix products  20.3 us (6%)
  between operations  13.4 us (4%)
  other arithmetic  11 us (3%)
  starting transfers between devices  7.65 us (2%)
    psum x1, waiting for transfers between devices, body(): summed = lax.psum(summed, 'seq')  77.4 us
    psum x1, waiting for transfers between devices, body(): mixed = lax.psum(partial, 'seq')  72.8 us
    reduce_scatter x1, waiting for transfers between devices, body(): outputs = lax.psum_scatter(outputs, 'seq', scatter_dimension=1, tiled=True)  40.8 us
    reduce_scatter x1, waiting for transfers between devices, body(): summed = lax.psum_scatter(summed, 'req', scatter_dimension=0, tiled=True)  35.6 us
    psum x1, blocking collectives, body(): totals = lax.psum(jnp.sum(weights, axis=-1), 'seq').reshape(rows, H)  21 us
    all_gather x1, waiting for transfers between devices, body(): block_rows = lax.all_gather(feed_input, 'req', axis=0, tiled=True)  17.7 us
    unnamed x26, local copies, waits for them, and re-layouts  12.2 us
    ppermute x3, starting transfers between devices, body(): lax.ppermute(projected, 'seq', [(j0, j0 ^ g_now) for j0 in range(built)])  7.48 us
  transfers between devices with their start and end apart: 8, of which 8 were waited for; matrix products, arithmetic and copies ran while one was open for 5% of the time, Pallas kernels for 0%

profile of v1, /device:TPU:0, one launch (start us, length us, event | category | flops | bytes accessed | tf_op | source)
XLA Modules:
  0.0 356.8 jit_solution(6538524719189028177)
XLA Ops:
  6.5 2.1 copy.64
  9.9 2.1 reshape.160
  12.2 4.8 %convolution_convert_fusion = bf16[48,1024]{1,0:T(8,128)(2,1)S(1)} fusion(bf16[3584,1024]{1,0:T(8,128)(2,1)} %param.21, f32[48,3584]{1,0:T(8,128)} %reshape.160, f32[3584]{0:T(1024)S(1)} %copy-done.4, f32[48]{0:T(128)S(1)} %rsqrt.36), kind=kOutput, calls=%fused_computation.14 | convolution fusion | flops 352886784 | bytes 8140992 | tf_op jit(solution)/shard_map/dot_general | solution.py:85
  17.0 3.0 collective-permute-start
  20.8 2.1 collective-permute-done
  22.9 2.0 collective-permute-start.1
  24.9 4.2 %collective-permute-done.1 = bf16[48,2048]{1,0:T(8,128)(2,1)S(1)} collective-permute-done((bf16[48,2048]{1,0:T(8,128)(2,1)S(1)}, bf16[48,2048]{1,0:T(8,128)(2,1)S(1)}, u32[]{:S(2)}, u32[]{:S(2)}) %collective-permute-start.1) | collective-permute-done | bytes 196640 | tf_op jit(solution)/shard_map/ppermute | solution.py:91
  29.9 2.5 collective-permute-start.2
  32.4 3.9 %copy.69 = bf16[1,512,2048]{1,2,0:T(8,128)(2,1)} copy(bf16[1,512,2048]{2,1,0:T(8,128)(2,1)} %param.16) | data formatting | bytes 4194304 | tf_op args[1]
  36.3 3.9 %copy.72 = bf16[512,8,256]{2,0,1:T(8,128)(2,1)} copy(bf16[512,8,256]{0,2,1:T(8,128)(2,1)} %bitcast.44) | data formatting | bytes 4194304 | tf_op jit(solution)/shard_map/reshape;squeeze | solution.py:78
  40.2 3.9 %copy.65 = bf16[1,512,2048]{1,2,0:T(8,128)(2,1)} copy(bf16[1,512,2048]{2,1,0:T(8,128)(2,1)} %param.17) | data formatting | bytes 4194304 | tf_op args[2]
  44.2 3.9 %copy.67 = bf16[512,8,256]{2,0,1:T(8,128)(2,1)} copy(bf16[512,8,256]{0,2,1:T(8,128)(2,1)} %bitcast.45) | data formatting | bytes 4194304 | tf_op jit(solution)/shard_map/reshape;squeeze | solution.py:79
  48.9 1.6 maximum_select_fusion
  56.3 2.7 reshape.156
  59.1 21.0 %psum.21 = f32[48,16]{0,1:T(8,128)S(1)} all-reduce(f32[48,16]{0,1:T(8,128)S(1)} %bitcast.56), channel_id=1, replica_groups=mesh['req'=4,'seq'=8] {'seq'}, use_global_device_ids=true, to_apply=%region_4.5 | all-reduce | flops 768 | bytes 6144 | tf_op jit(solution)/shard_map/psum | solution.py:116
  81.7 40.8 %reduce-scatter.3.cloned.1.call-done = f32[48,512]{1,0:T(8,128)} async-done(((f32[48,4096]{1,0:T(8,128)}), f32[48,512]{1,0:T(8,128)}) %reduce-scatter.3.cloned.1.call-update) | async-done | bytes 98320 | tf_op jit(solution)/shard_map/reduce_scatter | solution.py:123
  122.5 3.8 %fusion.29 = f32[48,3584]{1,0:T(8,128)} fusion(bf16[512,3584]{1,0:T(8,128)(2,1)} %param.22, f32[48,512]{1,0:T(8,128)} %reduce-scatter.3.cloned.1.call-done, f32[48,4096]{1,0:T(8,128)} %bitcast.51, s32[]{:T(128)S(6)} %select_n.47), kind=kOutput, calls=%fused_computation.54 | convolution fusion | flops 176209920 | bytes 4554756 | tf_op jit(solution)/shard_map/dot_general | solution.py:127
  126.3 72.8 %all-reduce.3.cloned.1.call-done = f32[48,3584]{1,0:T(8,128)} async-done(((f32[48,3584]{1,0:T(8,128)}), f32[48,3584]{1,0:T(8,128)}) %all-reduce.3.cloned.1.call-update) | async-done | bytes 688144 | tf_op jit(solution)/shard_map/psum | solution.py:128
  203.8 17.7 %all-gather.2.cloned.1.call-done = bf16[192,3584]{1,0:T(8,128)(2,1)} async-done(((bf16[48,3584]{1,0:T(8,128)(2,1)}), bf16[192,3584]{1,0:T(8,128)(2,1)}) %all-gather.2.cloned.1.call-update) | async-done | bytes 1376272 | tf_op jit(solution)/shard_map/all_gather | solution.py:131
  221.5 4.2 %fusion.41 = f32[192,448]{1,0:T(8,128)} fusion(bf16[192,3584]{1,0:T(8,128)(2,1)} %all-gather.2.cloned.1.call-done, bf16[3584,448]{0,1:T(8,128)(2,1)} %param.23), kind=kOutput, calls=%fused_computation.78 | convolution fusion | flops 616562688 | bytes 4931584 | tf_op jit(solution)/shard_map/dot_general | solution.py:132
  225.6 6.0 %fusion.10 = f32[192,3584]{1,0:T(8,128)} fusion(bf16[448,3584]{1,0:T(8,128)(2,1)S(1)} %copy-done, bf16[192,3584]{1,0:T(8,128)(2,1)} %all-gather.2.cloned.1.call-done, bf16[3584,448]{0,1:T(8,128)(2,1)} %param.24, f32[192,448]{1,0:T(8,128)} %fusion.41), kind=kOutput, calls=%fused_computation.15 | convolution fusion | flops 1233985536 | bytes 10895360 | tf_op jit(solution)/shard_map/dot_general | solution.py:135
  231.7 35.6 %reduce-scatter.5.cloned.1.call-done = f32[48,3584]{1,0:T(8,128)} async-done(((f32[192,3584]{1,0:T(8,128)}), f32[48,3584]{1,0:T(8,128)}) %reduce-scatter.5.cloned.1.call-update) | async-done | bytes 688144 | tf_op jit(solution)/shard_map/reduce_scatter | solution.py:136
  267.3 77.4 %all-reduce.5.cloned.1.call-done = f32[48,3584]{1,0:T(8,128)} async-done(((f32[48,3584]{1,0:T(8,128)}), f32[48,3584]{1,0:T(8,128)}) %all-reduce.5.cloned.1.call-update) | async-done | bytes 688144 | tf_op jit(solution)/shard_map/psum | solution.py:137
  348.3 2.0 copy.77
  (76 shorter events, 19.6 us)
Async XLA Ops:
  6.5 219.1 %copy-start = (bf16[448,3584]{1,0:T(8,128)(2,1)S(1)}, bf16[448,3584]{1,0:T(8,128)(2,1)}, u32[]{:S(2)}) copy-start(bf16[448,3584]{1,0:T(8,128)(2,1)} %param.25) | copy-start | bytes 9633796
  6.5 5.7 %copy-start.4 = (f32[3584]{0:T(1024)S(1)}, f32[3584]{0:T(1024)}, u32[]{:S(2)}) copy-start(f32[3584]{0:T(1024)} %param.26) | copy-start | bytes 43012
  6.5 115.9 %reduce-scatter.3.cloned.1.call-start = ((), (), s32[]{:S(2)}) async-start(), calls=%async_computation.2 | async-start | bytes 884736 | tf_op jit(solution)/shard_map/reduce_scatter | solution.py:123
  12.2 8.0 %copy-start.8 = (s32[48]{0:T(128)S(1)}, s32[48]{0:T(128)}, u32[]{:S(2)}) copy-start(s32[48]{0:T(128)} %param.19) | copy-start | bytes 580
  12.2 8.1 %copy-start.7 = (s32[1,512]{1,0:T(1,128)S(1)}, s32[1,512]{1,0:T(1,128)}, u32[]{:S(2)}) copy-start(s32[1,512]{1,0:T(1,128)} %param.18) | copy-start | bytes 6148
  12.2 8.2 %copy-start.9 = (s32[48]{0:T(128)S(1)}, s32[48]{0:T(128)}, u32[]{:S(2)}) copy-start(s32[48]{0:T(128)} %param.20) | copy-start | bytes 580
  17.0 5.8 %collective-permute-start = (bf16[48,1024]{1,0:T(8,128)(2,1)S(1)}, bf16[48,1024]{1,0:T(8,128)(2,1)S(1)}, u32[]{:S(2)}, u32[]{:S(2)}) collective-permute-start(bf16[48,1024]{1,0:T(8,128)(2,1)S(1)} %convolution_convert_fusion), channel_id=1, source_target_pairs={{0,1},{1,0},{2,3},{3,2},{4,5},{5,4},{6,7},{7,6},{8,9},{9,8},{10,11... | collective-permute-start | bytes 294920 | tf_op jit(solution)/shard_map/ppermute | solution.py:91
  22.9 6.2 %collective-permute-start.1 = (bf16[48,2048]{1,0:T(8,128)(2,1)S(1)}, bf16[48,2048]{1,0:T(8,128)(2,1)S(1)}, u32[]{:S(2)}, u32[]{:S(2)}) collective-permute-start(bf16[48,2048]{1,0:T(8,128)(2,1)S(1)} %maximum_select_fusion.2), channel_id=1, source_target_pairs={{0,2},{1,3},{2,0},{3,1},{4,6},{5,7},{6,4},{7,5},{8,10},{9,11},{10,... | collective-permute-start | bytes 589832 | tf_op jit(solution)/shard_map/ppermute | solution.py:91
  29.9 19.0 %collective-permute-start.2 = (bf16[48,4096]{1,0:T(8,128)(2,1)}, bf16[48,4096]{1,0:T(8,128)(2,1)}, u32[]{:S(2)}, u32[]{:S(2)}) collective-permute-start(bf16[48,4096]{1,0:T(8,128)(2,1)} %maximum_select_fusion.1), channel_id=1, source_target_pairs={{0,4},{1,5},{2,6},{3,7},{4,0},{5,1},{6,2},{7,3},{8,12},{9,13},{10,... | collective-permute-start | bytes 1179656 | tf_op jit(solution)/shard_map/ppermute | solution.py:91
  51.1 1.6 copy-start.3
  52.7 1.6 copy-start.2
  59.0 140.1 %all-reduce.3.cloned.1.call-start = ((), (), s32[]{:S(2)}) async-start(), calls=%async_computation.3 | async-start | bytes 1376256 | tf_op jit(solution)/shard_map/psum | solution.py:128
  122.5 77.9 %copy-start.6 = (f32[3584]{0:T(1024)S(1)}, f32[3584]{0:T(1024)}, u32[]{:S(2)}) copy-start(f32[3584]{0:T(1024)} %param.27) | copy-start | bytes 43012
  126.2 76.6 %copy-start.5 = (f32[3584]{0:T(1024)S(1)}, f32[3584]{0:T(1024)}, u32[]{:S(2)}) copy-start(f32[3584]{0:T(1024)} %param.28) | copy-start | bytes 43012
  126.3 95.2 %all-gather.2.cloned.1.call-start = ((), (), s32[]{:S(2)}) async-start(), calls=%async_computation.4 | async-start | bytes 1720320 | tf_op jit(solution)/shard_map/all_gather | solution.py:131
  202.0 0.9 copy-start.1
  203.8 63.5 %reduce-scatter.5.cloned.1.call-start = ((), (), s32[]{:S(2)}) async-start(), calls=%async_computation.5 | async-start | bytes 3440640 | tf_op jit(solution)/shard_map/reduce_scatter | solution.py:136
  231.7 113.0 %all-reduce.5.cloned.1.call-start = ((), (), s32[]{:S(2)}) async-start(), calls=%async_computation.6 | async-start | bytes 1376256 | tf_op jit(solution)/shard_map/psum | solution.py:137
Sparse Core Ops, SparseCore 0:
  59.1 63.2 reduce-scatter.2
  126.4 72.7 all-reduce.2
  203.9 17.5 all-gather.1
  231.8 35.4 reduce-scatter.4
  270.9 73.6 all-reduce.4
